TPU v7x, 32 devices: a whole 2x2x4 slice. The times are simulated.
32 devices in a mesh: blk: 8 (over y, x, core), expert: 4 (over z).
Axes of the slice: x: 2, y: 2, z: 4, core: 2. Of those that a mesh axis runs over, the one named last changes fastest.
Arguments:
- residual: bfloat16 [2048, 4096], P('blk', 'expert'), may hold values from -3 to 3
- queries: bfloat16 [2048, 2048], P('blk', 'expert'), may hold values from -8 to 8
- key_cache: bfloat16 [2048, 1024], P('blk', 'expert'), may hold values from -8 to 8
- value_cache: bfloat16 [2048, 1024], P('blk', 'expert'), may hold values from -6 to 6
- segments: int32 [2048], replicated, may hold values from 0 to 3, never falling along the last dimension, each value on 1 to 1536 neighbouring positions
- routes: int32 [2048, 2], P('blk'), may hold values from 0 to 3, all different within a row; in each aligned block of 256 rows (0 to 255, 256 to 511, ...) at most 144 rows name the same one
- w_out: bfloat16 [2048, 4096], P('expert'), may hold values from -0.125 to 0.125
- norm_gain: float32 [4096], replicated, may hold values from 0.5 to 1.5
- w_router: bfloat16 [4096, 4], replicated, may hold values from -0.09375 to 0.09375
- w_gate: bfloat16 [4, 4096, 14336], P('expert', None, 'blk'), may hold values from -0.09375 to 0.09375
- w_up: bfloat16 [4, 4096, 14336], P('expert', None, 'blk'), may hold values from -0.09375 to 0.09375
- w_down: bfloat16 [4, 14336, 4096], P('expert', 'blk'), may hold values from -0.046875 to 0.046875
Outputs:
- layer_out: bfloat16 [2048, 4096], P(('blk', 'expert'))
Inputs may be any that keep to these rules, and one draw needn't show every extreme that they name: `segments`: segment ids never fall; one document holds exactly 1536 tokens and none holds more. `routes`: A token's 2 experts differ. In each aligned block of 256 rows (the tokens of one index of blk) no expert is named by more than 144 rows, a bound that some block reaches.
All inputs are finite; a program needn't handle non-finite values.
Results may differ from a plain program's by a relative error of at most 0.019.
Values may be sent and summed in bfloat16 or wider, within the bound.
A program may use at most 192 MiB of HBM per device.

v0:
```python
import math

import jax
import jax.numpy as jnp
from jax import lax
from jax.sharding import PartitionSpec as P

H = 16
KVH = 8
HD = 128
TOP = 2


def on_device(
    residual,
    queries,
    key_cache,
    value_cache,
    segments,
    routes,
    w_out,
    norm_gain,
    w_router,
    w_gate,
    w_up,
    w_down,
):
    tok_rows = queries.shape[0]
    kv_heads = key_cache.shape[1] // HD
    q_per_kv = H // KVH
    seq_block = lax.axis_index("blk")
    head_group = lax.axis_index("expert")
    group_count = lax.axis_size("expert")
    first_row = seq_block * tok_rows
    query_pos = first_row + jnp.arange(tok_rows, dtype=jnp.int32)
    query_seg = lax.dynamic_slice_in_dim(segments, first_row, tok_rows)
    query_four = queries.reshape(tok_rows, kv_heads, q_per_kv, HD)
    score_scale = 1.0 / math.sqrt(HD)
    running = jnp.full((kv_heads, q_per_kv, tok_rows), -1e30, jnp.float32)
    key_rows = lax.all_gather(key_cache, "blk", axis=0, tiled=True)
    value_rows = lax.all_gather(value_cache, "blk", axis=0, tiled=True)
    piece_len = key_rows.shape[0]
    key_pos = jnp.arange(piece_len, dtype=jnp.int32)
    visible = (query_seg[:, None] == segments[None, :]) & (key_pos[None, :] <= query_pos[:, None])
    scores = (
        jnp.einsum(
            "qkgd,skd->kgqs",
            query_four,
            key_rows.reshape(piece_len, kv_heads, HD),
            preferred_element_type=jnp.float32,
        )
        * score_scale
    )
    scores = jnp.where(visible, scores, -1e30)
    newmax = jnp.maximum(running, jnp.max(scores, axis=-1))
    weights = jnp.where(visible, jnp.exp(scores - newmax[..., None]), 0.0)
    totals = jnp.sum(weights, axis=-1)
    weighted_sum = jnp.einsum(
        "kgqs,skd->kgqd",
        weights.astype(jnp.bfloat16),
        value_rows.reshape(piece_len, kv_heads, HD),
        preferred_element_type=jnp.float32,
    )
    running, totals, weighted_sum = (newmax, totals, weighted_sum)
    attended = (
        jnp.transpose(weighted_sum / totals[..., None], (2, 0, 1, 3))
        .reshape(tok_rows, kv_heads * q_per_kv * HD)
        .astype(jnp.bfloat16)
    )
    head_term = jnp.dot(attended, w_out, preferred_element_type=jnp.float32)
    feat_width = residual.shape[1]
    own_cols = lax.dynamic_slice_in_dim(
        head_term, head_group * feat_width, feat_width, 1
    ) + residual.astype(jnp.float32)
    head_term = lax.dynamic_update_slice_in_dim(head_term, own_cols, head_group * feat_width, 1)
    row_share = tok_rows // group_count
    summed = lax.psum(head_term.astype(jnp.bfloat16), "expert").astype(jnp.float32)
    normed = (
        summed * lax.rsqrt(jnp.mean(summed * summed, axis=-1, keepdims=True) + 1e-05) * norm_gain
    ).astype(jnp.bfloat16)
    own_rows = lax.dynamic_slice_in_dim(summed, head_group * row_share, row_share, 0)
    gate_score = jax.nn.sigmoid(jnp.dot(normed, w_router, preferred_element_type=jnp.float32))
    picked = routes[:, :, None] == jnp.arange(w_router.shape[1], dtype=jnp.int32)[None, None, :]
    chosen = jnp.sum(jnp.where(picked, gate_score[:, None, :], 0.0), axis=-1)
    mixing = chosen / jnp.sum(chosen, axis=-1, keepdims=True)
    expert_id = head_group * w_gate.shape[0]
    chosen_here = routes == expert_id
    routed = jnp.any(chosen_here, axis=-1)
    share_w = jnp.sum(jnp.where(chosen_here, mixing, 0.0), axis=-1)
    capacity = tok_rows * TOP * 9 // (8 * w_gate.shape[0] * group_count)
    slot_index = jnp.cumsum(routed.astype(jnp.int32)) - 1
    placing = (
        (slot_index[None, :] == jnp.arange(capacity, dtype=jnp.int32)[:, None]) & routed[None, :]
    ).astype(jnp.bfloat16)
    buffer = jnp.dot(placing, normed, preferred_element_type=jnp.float32).astype(jnp.bfloat16)
    gate_w = w_gate[0]
    up_w = w_up[0]
    down_w = w_down[0]
    piece = lax.all_gather(buffer, "blk", axis=0, tiled=True)
    gate = jnp.dot(piece, gate_w, preferred_element_type=jnp.float32)
    up_proj = jnp.dot(piece, up_w, preferred_element_type=jnp.float32)
    hidden = (jax.nn.silu(gate) * up_proj).astype(jnp.bfloat16)
    expert_out = lax.psum_scatter(
        jnp.dot(hidden, down_w, preferred_element_type=jnp.float32).astype(jnp.bfloat16),
        "blk",
        scatter_dimension=0,
        tiled=True,
    ).astype(jnp.float32)
    contrib = jnp.take(expert_out, jnp.clip(slot_index, 0, capacity - 1), axis=0) * share_w[:, None]
    combined = lax.psum_scatter(
        contrib.astype(jnp.bfloat16), "expert", scatter_dimension=0, tiled=True
    ).astype(jnp.float32)
    return (own_rows + combined).astype(jnp.bfloat16)


def solution(mesh):
    return jax.shard_map(
        on_device,
        mesh=mesh,
        in_specs=(
            P("blk", "expert"),
            P("blk", "expert"),
            P("blk", "expert"),
            P("blk", "expert"),
            P(),
            P("blk", None),
            P("expert", None),
            P(),
            P(),
            P("expert", None, "blk"),
            P("expert", None, "blk"),
            P("expert", "blk", None),
        ),
        out_specs=P(("blk", "expert"), None),
        check_vma=False,
    )
```

profile of v0, /device:TPU:0, one launch (start us, length us, event | category | flops | bytes accessed | tf_op | source)
XLA Modules:
  0.0 430.6 jit_solution(4184735980926724905)
XLA Ops:
  6.5 0.0 copy-start
  6.5 0.0 all-gather.4.cloned.1.call-start
  6.5 1.7 copy.25
  8.2 0.0 all-gather.4.cloned.1.call-update
  8.2 0.0 all-gather.6.cloned.1.call-start
  8.3 0.7 all-gather.6.cloned.1.call-update
  9.0 0.0 all-reduce.2.cloned.1.call-start
  9.1 1.0 reshape.109
  10.1 0.8 dynamic_slice.9
  10.8 1.2 fusion.17
  12.1 23.5 %all-gather.4.cloned.1.call-done = bf16[2048,256]{0,1:T(8,128)(2,1)} async-done(((bf16[256,256]{0,1:T(8,128)(2,1)}), bf16[2048,256]{0,1:T(8,128)(2,1)}) %all-gather.4.cloned.1.call-update) | async-done | bytes 1048592 | tf_op jit(solution)/shard_map/all_gather | solution.py:40
  35.5 2.9 fusion.11
  38.4 0.0 copy-start.1
  38.4 3.2 copy-done.1
  41.6 2.1 fusion.12
  43.7 17.2 %all-gather.6.cloned.1.call-done = bf16[2048,256]{1,0:T(8,128)(2,1)} async-done(((bf16[256,256]{1,0:T(8,128)(2,1)}), bf16[2048,256]{1,0:T(8,128)(2,1)}) %all-gather.6.cloned.1.call-update) | async-done | bytes 1048592 | tf_op jit(solution)/shard_map/all_gather | solution.py:41
  61.0 1.5 copy.28
  62.4 0.0 copy-start.2
  62.5 5.7 %fusion.27 = bf16[256,2,2,128]{0,3,2,1:T(8,128)(2,1)S(1)} fusion(bf16[2048,2,128,1]{0,2,3,1:T(8,128)(2,1)S(1)} %bitcast.64, f32[2,2048,256,2]{2,1,3,0:T(8,128)} %copy-done.1, f32[2,2,256]{2,1,0:T(2,128)S(1)} %broadcast_maximum_fusion, pred[256,2048]{0,1:T(8,128)(4,1)S(1)} %fusion.17, f32[256,2,2]{0,2,1:T(2,128)S(1)} %bitcast.66), kind=kOutput, calls=%fused_computation.30 | convolution fusion | flops 547618816 | bytes 10231808 | tf_op jit(solution)/shard_map/kgqs,skd->kgqd/dot_general | solution.py:58
  68.2 0.0 copy-done.2
  68.2 0.0 copy-start.5
  68.2 1.3 fusion.44
  69.5 0.0 copy-done.5
  69.5 0.2 add_dynamic-update-slice_fusion
  69.8 0.0 copy-start.6
  69.8 0.0 copy-start.7
  69.8 1.6 convert_element_type.54
  71.4 0.0 all-reduce.2.cloned.1.call-update
  71.4 0.0 all-gather.8.cloned.1.call-start
  71.5 0.0 copy-done.6
  71.5 0.3 reduce-window.9
  71.8 0.1 slice.7
  71.9 0.1 slice_reduce_fusion
  72.1 0.1 compare_and_fusion
  72.1 86.0 %all-reduce.2.cloned.1.call-done = bf16[256,4096]{1,0:T(8,128)(2,1)} async-done(((bf16[256,4096]{1,0:T(8,128)(2,1)}), bf16[256,4096]{1,0:T(8,128)(2,1)}) %all-reduce.2.cloned.1.call-update) | async-done | bytes 2097168 | tf_op jit(solution)/shard_map/psum | solution.py:77
  158.1 2.1 multiply_reduce_fusion
  160.2 0.0 copy-done.7
  160.2 3.4 convolution_convert_fusion.1
  163.6 0.0 all-gather.8.cloned.1.call-update
  163.7 0.2 reduce-scatter.3.cloned.1.call-start
  163.9 57.7 %all-gather.8.cloned.1.call-done = bf16[1152,4096]{1,0:T(8,128)(2,1)} async-done(((bf16[144,4096]{1,0:T(8,128)(2,1)}), bf16[1152,4096]{1,0:T(8,128)(2,1)}) %all-gather.8.cloned.1.call-update) | async-done | bytes 9437200 | tf_op jit(solution)/shard_map/all_gather | solution.py:99
  221.6 0.0 slice-start
  221.6 25.3 %fusion.3 = f32[1152,1792]{1,0:T(8,128)} fusion(bf16[1152,4096]{1,0:T(8,128)(2,1)} %all-gather.8.cloned.1.call-done, bf16[1,4096,1792]{2,1,0:T(8,128)(2,1)} %param.21), kind=kOutput, calls=%fused_computation.5 | convolution fusion | flops 16911433728 | bytes 32374784 | tf_op jit(solution)/shard_map/dot_general | solution.py:100
  246.9 24.6 %fusion.8 = bf16[1152,1792]{1,0:T(8,128)(2,1)S(1)} fusion(bf16[1152,4096]{1,0:T(8,128)(2,1)} %all-gather.8.cloned.1.call-done, bf16[1,4096,1792]{2,1,0:T(8,128)(2,1)} %param.22, f32[1152,1792]{1,0:T(8,128)} %fusion.3), kind=kOutput, calls=%fused_computation.10 | convolution fusion | flops 16923820032 | bytes 36503552 | tf_op jit(solution)/shard_map/dot_general | solution.py:101
  271.5 0.0 slice-done
  271.5 0.0 slice-done.1
  271.5 0.0 slice-done.2
  271.5 0.0 slice-done.3
  271.6 19.5 %convolution_convert_fusion = bf16[1152,4096]{1,0:T(8,128)(2,1)} fusion(bf16[1152,1792]{1,0:T(8,128)(2,1)S(1)} %fusion.8, bf16[1,1792,4096]{2,1,0:T(8,128)(2,1)S(1)} %bitcast.70), kind=kOutput, calls=%fused_computation.1 | convolution fusion | flops 16916152320 | bytes 28246016 | tf_op jit(solution)/shard_map/dot_general | solution.py:104
  291.1 0.0 reduce-scatter.3.cloned.1.call-update
  291.1 0.3 reduce-scatter.5.cloned.1.call-start
  291.4 0.1 fusion.37
  291.5 0.0 copy-done
  291.5 1.2 copy-done.3
  292.7 0.7 fusion.23
  293.5 74.3 %reduce-scatter.3.cloned.1.call-done = bf16[144,4096]{1,0:T(8,128)(2,1)} async-done(((bf16[1152,4096]{1,0:T(8,128)(2,1)}), bf16[144,4096]{1,0:T(8,128)(2,1)}) %reduce-scatter.3.cloned.1.call-update) | async-done | bytes 1179664 | tf_op jit(solution)/shard_map/reduce_scatter | solution.py:103
  367.8 1.5 convert_element_type.62
  369.3 3.8 gather_fusion
  373.1 4.4 %multiply_convert_fusion = bf16[256,4096]{1,0:T(8,128)(2,1)} fusion(f32[256,4096]{1,0:T(8,128)} %gather_fusion, f32[256]{0:T(256)S(1)} %fusion.36, pred[256]{0:T(512)(128)(4,1)S(1)} %get-tuple-element.7), kind=kLoop, calls=%fused_computation.15 | loop fusion | flops 3145728 | bytes 6292736 | tf_op jit(solution)/shard_map/convert_element_type | solution.py:111
  377.5 0.0 reduce-scatter.5.cloned.1.call-update
  377.5 0.0 copy-done.4
  377.5 2.4 convert_element_type.55
  379.9 41.6 %reduce-scatter.5.cloned.1.call-done = bf16[64,4096]{1,0:T(8,128)(2,1)} async-done(((bf16[256,4096]{1,0:T(8,128)(2,1)}), bf16[64,4096]{1,0:T(8,128)(2,1)}) %reduce-scatter.5.cloned.1.call-update) | async-done | bytes 524304 | tf_op jit(solution)/shard_map/reduce_scatter | solution.py:110
  421.5 2.3 add_convert_fusion
  (16 shorter events, 0.2 us)
Async XLA Ops:
  6.5 284.9 %copy-start = (bf16[4096,4]{0,1:T(4,128)(2,1)S(1)}, bf16[4096,4]{0,1:T(4,128)(2,1)}, u32[]{:S(2)}) copy-start(bf16[4096,4]{0,1:T(4,128)(2,1)} %param.20) | copy-start | bytes 98308
  6.5 29.0 %all-gather.4.cloned.1.call-start = ((), (), s32[]{:S(2)}) async-start(), calls=%async_computation.2 | async-start | bytes 1179648 | tf_op jit(solution)/shard_map/all_gather | solution.py:40
  8.2 52.7 %all-gather.6.cloned.1.call-start = ((), (), s32[]{:S(2)}) async-start(), calls=%async_computation.3 | async-start | bytes 1179648 | tf_op jit(solution)/shard_map/all_gather | solution.py:41
  9.0 149.1 %all-reduce.2.cloned.1.call-start = ((), (), s32[]{:S(2)}) async-start(), calls=%async_computation.4 | async-start | bytes 4194304 | tf_op jit(solution)/shard_map/psum | solution.py:77
  38.4 3.2 copy-start.1
  62.4 5.8 %copy-start.2 = (bf16[512,4096]{1,0:T(8,128)(2,1)S(1)}, bf16[512,4096]{1,0:T(8,128)(2,1)}, u32[]{:S(2)}) copy-start(bf16[512,4096]{1,0:T(8,128)(2,1)} %param.18) | copy-start | bytes 12582916
  68.2 1.3 copy-start.5
  69.8 1.7 copy-start.6
  69.8 90.4 %copy-start.7 = (f32[4096]{0:T(1024)S(1)}, f32[4096]{0:T(1024)}, u32[]{:S(2)}) copy-start(f32[4096]{0:T(1024)} %param.19) | copy-start | bytes 49156
  71.4 150.2 %all-gather.8.cloned.1.call-start = ((), (), s32[]{:S(2)}) async-start(), calls=%async_computation.5 | async-start | bytes 10616832 | tf_op jit(solution)/shard_map/all_gather | solution.py:99
  163.7 204.1 %reduce-scatter.3.cloned.1.call-start = ((), (), s32[]{:S(2)}) async-start(), calls=%async_computation.6 | async-start | bytes 10616832 | tf_op jit(solution)/shard_map/reduce_scatter | solution.py:103
  221.6 49.9 %slice-start = ((s8[14680064]{0:T(1024)(128)(4,1)}), s8[4194304]{0:T(1024)(128)(4,1)S(1)}, s32[]{:S(2)}) async-start(s8[14680064]{0:T(1024)(128)(4,1)} %bitcast.69), calls=%async_computation.8 | async-start | bytes 8388608
  221.6 49.9 %slice-start.1 = ((s8[14680064]{0:T(1024)(128)(4,1)}), s8[4194304]{0:T(1024)(128)(4,1)S(1)}, s32[]{:S(2)}) async-start(s8[14680064]{0:T(1024)(128)(4,1)} %bitcast.69), calls=%async_computation.9 | async-start | bytes 8388608
  246.9 24.6 %slice-start.2 = ((s8[14680064]{0:T(1024)(128)(4,1)}), s8[4194304]{0:T(1024)(128)(4,1)S(1)}, s32[]{:S(2)}) async-start(s8[14680064]{0:T(1024)(128)(4,1)} %bitcast.69), calls=%async_computation.10 | async-start | bytes 8388608
  246.9 24.6 %slice-start.3 = ((s8[14680064]{0:T(1024)(128)(4,1)}), s8[2097152]{0:T(1024)(128)(4,1)S(1)}, s32[]{:S(2)}) async-start(s8[14680064]{0:T(1024)(128)(4,1)} %bitcast.69), calls=%async_computation.11 | async-start | bytes 4194304
  291.1 1.6 copy-start.3
  291.1 130.4 %reduce-scatter.5.cloned.1.call-start = ((), (), s32[]{:S(2)}) async-start(), calls=%async_computation.7 | async-start | bytes 2621440 | tf_op jit(solution)/shard_map/reduce_scatter | solution.py:110
  373.1 4.4 %copy-start.4 = (bf16[256,4096]{1,0:T(8,128)(2,1)S(1)}, bf16[256,4096]{1,0:T(8,128)(2,1)}, u32[]{:S(2)}) copy-start(bf16[256,4096]{1,0:T(8,128)(2,1)} %all-reduce.2.cloned.1.call-done) | copy-start | bytes 6291460
Sparse Core Ops, SparseCore 0:
  9.2 26.2 all-gather.3
  37.4 23.4 all-gather.5
  71.6 86.4 all-reduce.1
  163.8 57.7 all-gather.7
  291.2 76.5 reduce-scatter.2
  377.6 43.8 reduce-scatter.4
where the time goes:
time: 431 us
  waiting for transfers between devices  301 us (70%)
  matrix products  83.5 us (19%)
  other arithmetic  18.4 us (4%)
  between operations  13.7 us (3%)
  local copies, waits for them, and re-layouts  13.4 us (3%)
    psum x1, waiting for transfers between devices, on_device(): lax.psum(head_term.astype(jnp.bfloat16), 'expert').astype(jnp.float32)  86 us
    reduce_scatter x1, waiting for transfers between devices, on_device(): lax.psum_scatter(jnp.dot(hidden, down_w, preferred_element_type=jnp.float...  74.3 us
    all_gather x1, waiting for transfers between devices, on_device(): piece = lax.all_gather(buffer, 'blk', axis=0, tiled=True)  57.7 us
    reduce_scatter x1, waiting for transfers between devices, on_device(): lax.psum_scatter(contrib.astype(jnp.bfloat16), 'expert', scatter_dimensio...  41.6 us
    dot_general x1, matrix products, on_device(): gate = jnp.dot(piece, gate_w, preferred_element_type=jnp.float32)  25.3 us
    dot_general x1, matrix products, on_device(): up_proj = jnp.dot(piece, up_w, preferred_element_type=jnp.float32)  24.6 us
    all_gather x1, waiting for transfers between devices, on_device(): key_rows = lax.all_gather(key_cache, 'blk', axis=0, tiled=True)  23.5 us
    dot_general x1, matrix products, on_device(): jnp.dot(hidden, down_w, preferred_element_type=jnp.float32)  19.5 us
  transfers between devices with their start and end apart: 6, of which 6 were waited for; matrix products, arithmetic and copies ran while one was open for 3% of the time, Pallas kernels for 0%

commit v1 on v0

--- a/solution.py
+++ b/solution.py
@@ -1,14 +1,269 @@
+import functools
 import math
 
 import jax
 import jax.numpy as jnp
 from jax import lax
+from jax.experimental import pallas as pl
+from jax.experimental.pallas import tpu as pltpu
 from jax.sharding import PartitionSpec as P
 
 H = 16
 KVH = 8
 HD = 128
 TOP = 2
+
+MESH = pl.DeviceIdType.MESH
+
+
+def remote(src, dst, send_sem, recv_sem, target):
+    return pltpu.make_async_remote_copy(
+        src_ref=src,
+        dst_ref=dst,
+        send_sem=send_sem,
+        recv_sem=recv_sem,
+        device_id={"blk": target},
+        device_id_type=MESH,
+    )
+
+
+def enter(chips, chip, core):
+    barrier = pltpu.get_barrier_semaphore()
+    pl.semaphore_signal(barrier, inc=1, device_id={"blk": chip * 2 + 1 - core}, device_id_type=MESH)
+    for j in range(1, chips):
+        other = (chip + j) % chips
+        pl.semaphore_signal(barrier, inc=1, device_id={"blk": other * 2 + core}, device_id_type=MESH)
+    pl.semaphore_wait(barrier, chips)
+
+
+def gather_kernel(chips, k_ref, v_ref, ko_ref, vo_ref, send, recv, fsend, frecv, local):
+    me = lax.axis_index("blk")
+    chip, core = me // 2, me % 2
+    sibling = chip * 2 + 1 - core
+    pairs = ((k_ref, ko_ref), (v_ref, vo_ref))
+    enter(chips, chip, core)
+    out = []
+    for j in range(1, chips):
+        for i, (src, dst) in enumerate(pairs):
+            out.append(
+                remote(src, dst.at[me], send.at[i, j], recv.at[i, j], (chip + j) % chips * 2 + core)
+            )
+            out[-1].start()
+    for i, (src, dst) in enumerate(pairs):
+        out.append(remote(src, dst.at[me], fsend.at[i, 0], frecv.at[i, 0], sibling))
+        out[-1].start()
+    own = [pltpu.make_async_copy(src, dst.at[me], local.at[i]) for i, (src, dst) in enumerate(pairs)]
+    for copy in own:
+        copy.start()
+    for j in range(1, chips):
+        origin = (chip + chips - j) % chips * 2 + core
+        for i, (src, dst) in enumerate(pairs):
+            remote(src, dst.at[origin], send.at[i, j], recv.at[i, j], sibling).wait_recv()
+            out.append(
+                remote(dst.at[origin], dst.at[origin], fsend.at[i, j], frecv.at[i, j], sibling)
+            )
+            out[-1].start()
+    for j in range(chips):
+        origin = (chip + chips - j) % chips * 2 + 1 - core
+        for i, (src, dst) in enumerate(pairs):
+            remote(src, dst.at[origin], fsend.at[i, j], frecv.at[i, j], sibling).wait_recv()
+    for copy in own:
+        copy.wait()
+    for copy in out:
+        copy.wait_send()
+
+
+def gather_blocks(keys, values):
+    blocks = lax.axis_size("blk")
+    chips = blocks // 2
+    vmem = pl.BlockSpec(memory_space=pltpu.VMEM)
+    shape = jax.ShapeDtypeStruct((blocks,) + keys.shape, keys.dtype)
+    dma = pltpu.SemaphoreType.DMA
+    k_all, v_all = pl.pallas_call(
+        functools.partial(gather_kernel, chips),
+        out_shape=(shape, shape),
+        in_specs=[vmem, vmem],
+        out_specs=(vmem, vmem),
+        scratch_shapes=[dma((2, chips)), dma((2, chips)), dma((2, chips)), dma((2, chips)), dma((2,))],
+        compiler_params=pltpu.CompilerParams(collective_id=0, has_side_effects=True),
+    )(keys, values)
+    rows = blocks * keys.shape[0]
+    return k_all.reshape(rows, keys.shape[1]), v_all.reshape(rows, keys.shape[1])
+
+
+def expert_kernel(
+    chips,
+    tiles,
+    x_ref,
+    wg_ref,
+    wu_ref,
+    wd_ref,
+    o_ref,
+    rows_in,
+    acc,
+    keep,
+    leaving,
+    sib_in,
+    part_in,
+    ag_send,
+    ag_recv,
+    fw_send,
+    fw_recv,
+    sib_send,
+    sib_recv,
+    rs_send,
+    rs_recv,
+    local,
+):
+    j, f = pl.program_id(0), pl.program_id(1)
+    me = lax.axis_index("blk")
+    chip, core = me // 2, me % 2
+    sibling = chip * 2 + 1 - core
+    rows, width = x_ref.shape
+    mid = min(2, tiles - 1)
+
+    def push(k):
+        return remote(
+            rows_in.at[0, 0], rows_in.at[k, 0], ag_send.at[k], ag_recv.at[k], (chip + k) % chips * 2 + core
+        )
+
+    def forward(k):
+        return remote(rows_in.at[k, 0], rows_in.at[k, 1], fw_send.at[k], fw_recv.at[k], sibling)
+
+    def exchange(k):
+        return remote(leaving.at[k % 2], sib_in.at[k], sib_send.at[k], sib_recv.at[k], sibling)
+
+    def deliver(k):
+        return remote(
+            sib_in.at[k], part_in.at[k], rs_send.at[k], rs_recv.at[k], (chip + chips - k) % chips * 2 + core
+        )
+
+    @pl.when((j == 0) & (f == 0))
+    def _():
+        own = pltpu.make_async_copy(x_ref, rows_in.at[0, 0], local)
+        own.start()
+        enter(chips, chip, core)
+        own.wait()
+        forward(0).start()
+        for k in range(1, min(3, chips)):
+            push(k).start()
+
+    @pl.when((j >= 1) & (f == 0) & (j + 2 < chips))
+    def _():
+        push(j + 2).start()
+
+    @pl.when(f == 0)
+    def _():
+        forward(j).wait_recv()
+
+    tokens = rows_in[j].reshape(2 * rows, width)
+    gate = jnp.dot(tokens, wg_ref[...], preferred_element_type=jnp.float32)
+    up = jnp.dot(tokens, wu_ref[...], preferred_element_type=jnp.float32)
+    hidden = (gate / (1.0 + jnp.exp(-gate)) * up).astype(jnp.bfloat16)
+    step = 1024
+
+    @pl.when(f == 0)
+    def _():
+        for c in range(0, width, step):
+            acc[:, c : c + step] = jnp.dot(
+                hidden, wd_ref[:, c : c + step], preferred_element_type=jnp.float32
+            )
+
+    @pl.when(f > 0)
+    def _():
+        for c in range(0, width, step):
+            acc[:, c : c + step] += jnp.dot(
+                hidden, wd_ref[:, c : c + step], preferred_element_type=jnp.float32
+            )
+
+    @pl.when((f == mid) & (j + 1 < chips))
+    def _():
+        push(j + 1).wait_recv()
+        forward(j + 1).start()
+
+    def settle(k):
+        exchange(k).wait_recv()
+        sib_in[k] = (keep[...] + sib_in[k].astype(jnp.float32)).astype(jnp.bfloat16)
+        deliver(k).start()
+
+    @pl.when((f == 1) & (j == 1))
+    def _():
+        exchange(0).wait_recv()
+        o_ref[...] += sib_in[0].astype(jnp.float32)
+
+    @pl.when((f == 1) & (j >= 2))
+    def _():
+        settle(j - 1)
+
+    @pl.when(f == tiles - 1)
+    def _():
+        @pl.when(j >= 2)
+        def _():
+            exchange(j - 2).wait_send()
+
+        leaving[j % 2] = acc[rows:, :].astype(jnp.bfloat16)
+        exchange(j).start()
+
+        @pl.when(j == 0)
+        def _():
+            o_ref[...] = acc[:rows, :]
+
+        @pl.when(j > 0)
+        def _():
+            keep[...] = acc[:rows, :]
+
+        @pl.when(j == chips - 1)
+        def _():
+            settle(chips - 1)
+            for k in range(1, chips):
+                deliver(k).wait_recv()
+                o_ref[...] += part_in[k].astype(jnp.float32)
+            for k in range(chips):
+                forward(k).wait_send()
+                if k >= 1:
+                    push(k).wait_send()
+                    deliver(k).wait_send()
+            for k in range(max(0, chips - 2), chips):
+                exchange(k).wait_send()
+
+
+def expert_layer(x, gate_w, up_w, down_w):
+    blocks = lax.axis_size("blk")
+    chips = blocks // 2
+    rows, width = x.shape
+    units = gate_w.shape[1]
+    tile = 256 if units % 256 == 0 else 128
+    tiles = units // tile
+    dma = pltpu.SemaphoreType.DMA
+    low, wide = jnp.bfloat16, jnp.float32
+    return pl.pallas_call(
+        functools.partial(expert_kernel, chips, tiles),
+        grid=(chips, tiles),
+        out_shape=jax.ShapeDtypeStruct((rows, width), wide),
+        in_specs=[
+            pl.BlockSpec(memory_space=pl.ANY),
+            pl.BlockSpec((width, tile), lambda j, f: (0, f)),
+            pl.BlockSpec((width, tile), lambda j, f: (0, f)),
+            pl.BlockSpec((tile, width), lambda j, f: (f, 0)),
+        ],
+        out_specs=pl.BlockSpec((rows, width), lambda j, f: (0, 0)),
+        scratch_shapes=[
+            pltpu.VMEM((chips, 2, rows, width), low),
+            pltpu.VMEM((2 * rows, width), wide),
+            pltpu.VMEM((rows, width), wide),
+            pltpu.VMEM((2, rows, width), low),
+            pltpu.VMEM((chips, rows, width), low),
+            pltpu.VMEM((chips, rows, width), low),
+        ]
+        + [dma((chips,)) for _ in range(8)]
+        + [dma],
+        compiler_params=pltpu.CompilerParams(
+            collective_id=1,
+            has_side_effects=True,
+            dimension_semantics=("arbitrary", "arbitrary"),
+            vmem_limit_bytes=60 * 1024 * 1024,
+        ),
+    )(x, gate_w, up_w, down_w)
 
 
 def on_device(
@@ -37,8 +292,7 @@
     query_four = queries.reshape(tok_rows, kv_heads, q_per_kv, HD)
     score_scale = 1.0 / math.sqrt(HD)
     running = jnp.full((kv_heads, q_per_kv, tok_rows), -1e30, jnp.float32)
-    key_rows = lax.all_gather(key_cache, "blk", axis=0, tiled=True)
-    value_rows = lax.all_gather(value_cache, "blk", axis=0, tiled=True)
+    key_rows, value_rows = gather_blocks(key_cache, value_cache)
     piece_len = key_rows.shape[0]
     key_pos = jnp.arange(piece_len, dtype=jnp.int32)
     visible = (query_seg[:, None] == segments[None, :]) & (key_pos[None, :] <= query_pos[:, None])
@@ -88,6 +342,7 @@
     routed = jnp.any(chosen_here, axis=-1)
     share_w = jnp.sum(jnp.where(chosen_here, mixing, 0.0), axis=-1)
     capacity = tok_rows * TOP * 9 // (8 * w_gate.shape[0] * group_count)
+    capacity = -(-capacity // 16) * 16
     slot_index = jnp.cumsum(routed.astype(jnp.int32)) - 1
     placing = (
         (slot_index[None, :] == jnp.arange(capacity, dtype=jnp.int32)[:, None]) & routed[None, :]
@@ -96,16 +351,7 @@
     gate_w = w_gate[0]
     up_w = w_up[0]
     down_w = w_down[0]
-    piece = lax.all_gather(buffer, "blk", axis=0, tiled=True)
-    gate = jnp.dot(piece, gate_w, preferred_element_type=jnp.float32)
-    up_proj = jnp.dot(piece, up_w, preferred_element_type=jnp.float32)
-    hidden = (jax.nn.silu(gate) * up_proj).astype(jnp.bfloat16)
-    expert_out = lax.psum_scatter(
-        jnp.dot(hidden, down_w, preferred_element_type=jnp.float32).astype(jnp.bfloat16),
-        "blk",
-        scatter_dimension=0,
-        tiled=True,
-    ).astype(jnp.float32)
+    expert_out = expert_layer(buffer, gate_w, up_w, down_w)
     contrib = jnp.take(expert_out, jnp.clip(slot_index, 0, capacity - 1), axis=0) * share_w[:, None]
     combined = lax.psum_scatter(
         contrib.astype(jnp.bfloat16), "expert", scatter_dimension=0, tiled=True

time: 431 us -> 357 us (0.83)
  waiting for transfers between devices: 301 us -> 127 us
  Pallas kernels: 0 us -> 166 us
  matrix products: 83.5 us -> 14.5 us
  other arithmetic: 18.4 us -> 23.8 us
    pallas_call x0 -> x2, Pallas kernels: none -> 166 us  [the longest x1 145 us: expert_layer(): pl.pallas_call(functools.partial(expert_kernel, chips, tiles), grid=(chip...]
    all_gather x3 -> x0, waiting for transfers between devices: 98.4 us -> none  [the longest x1 57.7 us: on_device(): piece = lax.all_gather(buffer, 'blk', axis=0, tiled=True)]
    reduce_scatter x1 -> x0, waiting for transfers between devices: 74.3 us -> none  [on_device(): lax.psum_scatter(jnp.dot(hidden, down_w, preferred_element_type=jnp.float...]
    dot_general x3 -> x0, matrix products: 69.4 us -> none  [the longest x1 25.3 us: on_device(): gate = jnp.dot(piece, gate_w, preferred_element_type=jnp.float32)]
    unnamed x25 -> x18, local copies, waits for them, and re-layouts: 6.12 us -> 1.22 us
  transfers between devices with their start and end apart: 6 -> 2, of which waited for: 6 -> 2; matrix products, arithmetic and copies ran while one was open for 3% -> 1% of each run, Pallas kernels for 0% -> 0%
where the time goes in v1:
time: 357 us; the launch traced here: 356 us
  Pallas kernels  166 us (46%)
  waiting for transfers between devices  127 us (36%)
  other arithmetic  23.8 us (7%)
  matrix products  14.5 us (4%)
  between operations  13.6 us (4%)
  local copies, waits for them, and re-layouts  12.1 us (3%)
    pallas_call x1, Pallas kernels, expert_layer(): pl.pallas_call(functools.partial(expert_kernel, chips, tiles), grid=(chip...  145 us
    psum x1, waiting for transfers between devices, on_device(): lax.psum(head_term.astype(jnp.bfloat16), 'expert').astype(jnp.float32)  86.6 us
    reduce_scatter x1, waiting for transfers between devices, on_device(): lax.psum_scatter(contrib.astype(jnp.bfloat16), 'expert', scatter_dimensio...  40.1 us
    pallas_call x1, Pallas kernels, gather_blocks(): pl.pallas_call(functools.partial(gather_kernel, chips), out_shape=(shape,...  20.1 us
    gather x1, local copies, waits for them, and re-layouts, on_device(): jnp.take(expert_out, jnp.clip(slot_index, 0, capacity - 1), axis=0)  7.28 us
  transfers between devices with their start and end apart: 2, of which 2 were waited for; matrix products, arithmetic and copies ran while one was open for 1% of the time, Pallas kernels for 0%

profile of v1, /device:TPU:0, one launch (start us, length us, event | category | flops | bytes accessed | tf_op | source)
XLA Modules:
  0.0 356.4 jit_solution(2979771091580125151)
XLA Ops:
  6.5 0.0 copy-start
  6.5 0.0 all-reduce.2.cloned.1.call-start
  6.5 20.1 %shard_map.118 = (bf16[8,256,256]{2,1,0:T(8,128)(2,1)}, bf16[8,256,256]{2,1,0:T(8,128)(2,1)}) custom-call(bf16[256,256]{1,0:T(8,128)(2,1)} %k_ref.1, bf16[256,256]{1,0:T(8,128)(2,1)} %v_ref.1), custom_call_target="tpu_custom_call" | custom-call | tf_op jit(solution)/shard_map/pallas_call | solution.py:82
  26.7 1.3 reshape_reshape.6
  28.0 1.0 reshape.102
  29.0 0.8 dynamic_slice.9
  29.8 1.2 fusion.6
  31.0 0.0 copy-start.5
  31.0 4.7 %fusion = (f32[2,2,256]{2,1,0:T(2,128)S(1)}, f32[2,2048,256,2]{2,1,3,0:T(8,128)}) fusion(pred[256,2048]{0,1:T(8,128)(4,1)S(1)} %fusion.6, bf16[256,2,2,128]{3,2,1,0:T(2,128)(2,1)S(1)} %reshape.102, bf16[2048,2,128,1]{2,1,0,3:T(2,128)(2,1)S(1)} %bitcast.44), kind=kOutput, calls=%fused_computation.3 | convolution fusion | flops 543161344 | bytes 10227712 | tf_op jit(solution)/shard_map/qkgd,skd->kgqs/dot_general | solution.py:300
  35.8 0.0 copy-done.5
  35.8 0.3 reshape_reshape.7
  36.1 0.0 copy-start.3
  36.1 4.6 %fusion.1 = f32[2,2,256]{2,1,0:T(2,128)S(1)} fusion(f32[2,2048,256,2]{2,1,3,0:T(8,128)} %get-tuple-element.14, f32[2,2,256]{2,1,0:T(2,128)S(1)} %broadcast_maximum_fusion, pred[256,2048]{0,1:T(8,128)(4,1)S(1)} %fusion.6), kind=kLoop, calls=%fused_computation.4 | loop fusion | flops 10484736 | bytes 8921088 | tf_op jit(solution)/shard_map/reduce_sum | solution.py:311
  40.7 1.2 copy-done.3
  41.9 0.0 copy-start.2
  41.9 2.4 fusion.21
  44.3 0.0 copy-done.2
  44.3 0.0 copy-start.6
  44.3 3.2 fusion.39
  47.6 0.0 copy-done.6
  47.6 2.4 add_dynamic-update-slice_fusion
  49.9 0.0 copy-start.7
  49.9 0.0 copy-start.8
  49.9 3.8 %convert_element_type.45 = bf16[256,4096]{1,0:T(8,128)(2,1)} convert(f32[256,4096]{1,0:T(8,128)} %add_dynamic-update-slice_fusion) | non-fusion elementwise | flops 1048576 | bytes 6291456 | tf_op jit(solution)/shard_map/convert_element_type | solution.py:331
  53.7 0.0 all-reduce.2.cloned.1.call-update
  53.8 0.2 reduce-scatter.2.cloned.1.call-start
  54.0 0.0 copy-done.7
  54.0 0.3 reduce-window.9
  54.3 0.1 slice.7
  54.5 0.1 slice_reduce_fusion
  54.6 0.1 fusion.32
  54.7 0.1 compare_and_fusion
  54.7 86.6 %all-reduce.2.cloned.1.call-done = bf16[256,4096]{1,0:T(8,128)(2,1)} async-done(((bf16[256,4096]{1,0:T(8,128)(2,1)}), bf16[256,4096]{1,0:T(8,128)(2,1)}) %all-reduce.2.cloned.1.call-update) | async-done | bytes 2097168 | tf_op jit(solution)/shard_map/psum | solution.py:331
  141.3 0.0 copy-start.4
  141.3 2.2 multiply_reduce_fusion
  143.5 0.0 copy-done
  143.5 0.0 copy-done.8
  143.6 2.3 fusion.12
  145.9 0.0 copy-done.4
  146.0 1.8 convolution_convert_fusion.x_ref
  147.8 145.4 %shard_map.119 = f32[144,4096]{1,0:T(8,128)} custom-call(bf16[144,4096]{1,0:T(8,128)(2,1)} %convolution_convert_fusion.x_ref, bf16[4096,1792]{1,0:T(8,128)(2,1)} %bitcast.40, bf16[4096,1792]{1,0:T(8,128)(2,1)} %bitcast.41, bf16[1792,4096]{1,0:T(8,128)(2,1)} %bitcast.42), custom_call_target="tpu_custom_call" | custom-call | tf_op jit(solution)/shard_map/pallas_call | solution.py:239
  293.2 7.3 %gather_fusion = f32[256,4096]{1,0:T(8,128)} fusion(f32[144,4096]{1,0:T(8,128)} %shard_map.119, s32[1024]{0:T(1024)S(1)} %pad_clamp_fusion), kind=kCustom, calls=%fused_computation | custom fusion | bytes 8389632 | tf_op jit(solution)/shard_map/jit(_take)/gather | solution.py:355
  300.5 4.2 %multiply_convert_fusion = bf16[256,4096]{1,0:T(8,128)(2,1)} fusion(f32[256,4096]{1,0:T(8,128)} %gather_fusion, f32[256]{0:T(256)S(1)} %fusion.31, pred[256]{0:T(512)(128)(4,1)S(1)} %get-tuple-element.11), kind=kLoop, calls=%fused_computation.7 | loop fusion | flops 3145728 | bytes 6292736 | tf_op jit(solution)/shard_map/convert_element_type | solution.py:357
  304.7 0.0 reduce-scatter.2.cloned.1.call-update
  304.7 0.0 copy-start.1
  304.7 2.4 convert_element_type.46
  307.2 40.1 %reduce-scatter.2.cloned.1.call-done = bf16[64,4096]{1,0:T(8,128)(2,1)} async-done(((bf16[256,4096]{1,0:T(8,128)(2,1)}), bf16[64,4096]{1,0:T(8,128)(2,1)}) %reduce-scatter.2.cloned.1.call-update) | async-done | bytes 524304 | tf_op jit(solution)/shard_map/reduce_scatter | solution.py:356
  347.3 2.3 add_convert_fusion
  349.6 0.0 copy-done.1
  (10 shorter events, 0.2 us)
Async XLA Ops:
  6.5 137.0 %copy-start = (bf16[4096,4]{0,1:T(4,128)(2,1)S(1)}, bf16[4096,4]{0,1:T(4,128)(2,1)}, u32[]{:S(2)}) copy-start(bf16[4096,4]{0,1:T(4,128)(2,1)} %param.20) | copy-start | bytes 98308
  6.5 134.8 %all-reduce.2.cloned.1.call-start = ((), (), s32[]{:S(2)}) async-start(), calls=%async_computation.1 | async-start | bytes 4194304 | tf_op jit(solution)/shard_map/psum | solution.py:331
  31.0 4.7 %copy-start.5 = (bf16[8,256,256]{2,1,0:T(8,128)(2,1)S(1)}, bf16[8,256,256]{2,1,0:T(8,128)(2,1)}, u32[]{:S(2)}) copy-start(bf16[8,256,256]{2,1,0:T(8,128)(2,1)} %get-tuple-element.8) | copy-start | bytes 3145732
  36.1 5.8 %copy-start.3 = (f32[2,2048,256,2]{2,1,3,0:T(8,128)S(1)}, f32[2,2048,256,2]{2,1,3,0:T(8,128)}, u32[]{:S(2)}) copy-start(f32[2,2048,256,2]{2,1,3,0:T(8,128)} %get-tuple-element.14) | copy-start | bytes 25165828
  41.9 2.4 copy-start.2
  44.3 3.3 copy-start.6
  49.9 4.1 %copy-start.7 = (s32[256,2]{0,1:T(2,128)S(1)}, s32[256,2]{0,1:T(2,128)}, u32[]{:S(2)}) copy-start(s32[256,2]{0,1:T(2,128)} %param.17) | copy-start | bytes 6148
  49.9 93.6 %copy-start.8 = (f32[4096]{0:T(1024)S(1)}, f32[4096]{0:T(1024)}, u32[]{:S(2)}) copy-start(f32[4096]{0:T(1024)} %param.19) | copy-start | bytes 49156
  53.8 293.5 %reduce-scatter.2.cloned.1.call-start = ((), (), s32[]{:S(2)}) async-start(), calls=%async_computation.2 | async-start | bytes 2621440 | tf_op jit(solution)/shard_map/reduce_scatter | solution.py:356
  141.3 4.7 %copy-start.4 = (bf16[256,4096]{1,0:T(8,128)(2,1)S(1)}, bf16[256,4096]{1,0:T(8,128)(2,1)}, u32[]{:S(2)}) copy-start(bf16[256,4096]{1,0:T(8,128)(2,1)} %all-reduce.2.cloned.1.call-done) | copy-start | bytes 6291460
  304.7 44.8 %copy-start.1 = (bf16[4096,4]{0,1:T(4,128)(2,1)S(1)}, bf16[4096,4]{0,1:T(4,128)(2,1)}, u32[]{:S(2)}) copy-start(bf16[4096,4]{0,1:T(4,128)(2,1)} %param.20) | copy-start | bytes 98308
Sparse Core Ops, SparseCore 0:
  53.9 87.3 all-reduce.1
  304.9 42.4 reduce-scatter.1

commit v2 on v1

--- a/solution.py
+++ b/solution.py
@@ -16,33 +16,57 @@
 MESH = pl.DeviceIdType.MESH
 
 
-def remote(src, dst, send_sem, recv_sem, target):
+def remote(src, dst, send_sem, recv_sem, target, axis="blk"):
     return pltpu.make_async_remote_copy(
         src_ref=src,
         dst_ref=dst,
         send_sem=send_sem,
         recv_sem=recv_sem,
-        device_id={"blk": target},
+        device_id={axis: target},
         device_id_type=MESH,
     )
 
 
-def enter(chips, chip, core):
+def enter(chips, chip, core, experts=1):
     barrier = pltpu.get_barrier_semaphore()
-    pl.semaphore_signal(barrier, inc=1, device_id={"blk": chip * 2 + 1 - core}, device_id_type=MESH)
+    if chips > 0:
+        pl.semaphore_signal(
+            barrier, inc=1, device_id={"blk": chip * 2 + 1 - core}, device_id_type=MESH
+        )
     for j in range(1, chips):
         other = (chip + j) % chips
         pl.semaphore_signal(barrier, inc=1, device_id={"blk": other * 2 + core}, device_id_type=MESH)
-    pl.semaphore_wait(barrier, chips)
-
-
-def gather_kernel(chips, k_ref, v_ref, ko_ref, vo_ref, send, recv, fsend, frecv, local):
+    for k in range(1, experts):
+        other = (lax.axis_index("expert") + k) % experts
+        pl.semaphore_signal(barrier, inc=1, device_id={"expert": other}, device_id_type=MESH)
+    pl.semaphore_wait(barrier, chips + experts - 1)
+
+
+def gather_kernel(
+    chips, experts, k_ref, v_ref, w_ref, ko_ref, vo_ref, wo_ref,
+    send, recv, fsend, frecv, local, wsend, wrecv,
+):
     me = lax.axis_index("blk")
     chip, core = me // 2, me % 2
     sibling = chip * 2 + 1 - core
     pairs = ((k_ref, ko_ref), (v_ref, vo_ref))
-    enter(chips, chip, core)
+    group = lax.axis_index("expert")
+    enter(chips, chip, core, experts)
     out = []
+    part, cols = wo_ref.shape[1], wo_ref.shape[2]
+    mine = pl.ds(pl.multiple_of(me * part, part), part)
+
+    def piece(k):
+        target = (group + k) % experts
+        return w_ref.at[mine, pl.ds(pl.multiple_of(target * cols, 128), cols)]
+
+    def lend(k):
+        return remote(
+            piece(k), wo_ref.at[group], wsend.at[k], wrecv.at[k], (group + k) % experts, "expert"
+        )
+
+    for k in range(1, experts):
+        lend(k).start()
     for j in range(1, chips):
         for i, (src, dst) in enumerate(pairs):
             out.append(
@@ -53,6 +77,7 @@
         out.append(remote(src, dst.at[me], fsend.at[i, 0], frecv.at[i, 0], sibling))
         out[-1].start()
     own = [pltpu.make_async_copy(src, dst.at[me], local.at[i]) for i, (src, dst) in enumerate(pairs)]
+    own.append(pltpu.make_async_copy(piece(0), wo_ref.at[group], local.at[2]))
     for copy in own:
         copy.start()
     for j in range(1, chips):
@@ -69,26 +94,251 @@
             remote(src, dst.at[origin], fsend.at[i, j], frecv.at[i, j], sibling).wait_recv()
     for copy in own:
         copy.wait()
+    for k in range(1, experts):
+        origin = (group + experts - k) % experts
+        remote(
+            piece(k), wo_ref.at[origin], wsend.at[k], wrecv.at[k], (group + k) % experts, "expert"
+        ).wait_recv()
+        lend(k).wait_send()
     for copy in out:
         copy.wait_send()
 
 
-def gather_blocks(keys, values):
-    blocks = lax.axis_size("blk")
+def gather_blocks(keys, values, w_out):
+    blocks, experts = lax.axis_size("blk"), lax.axis_size("expert")
     chips = blocks // 2
     vmem = pl.BlockSpec(memory_space=pltpu.VMEM)
     shape = jax.ShapeDtypeStruct((blocks,) + keys.shape, keys.dtype)
+    wshape = jax.ShapeDtypeStruct(
+        (experts, w_out.shape[0] // blocks, w_out.shape[1] // experts), w_out.dtype
+    )
     dma = pltpu.SemaphoreType.DMA
-    k_all, v_all = pl.pallas_call(
-        functools.partial(gather_kernel, chips),
-        out_shape=(shape, shape),
-        in_specs=[vmem, vmem],
-        out_specs=(vmem, vmem),
-        scratch_shapes=[dma((2, chips)), dma((2, chips)), dma((2, chips)), dma((2, chips)), dma((2,))],
+    k_all, v_all, w_part = pl.pallas_call(
+        functools.partial(gather_kernel, chips, experts),
+        out_shape=(shape, shape, wshape),
+        in_specs=[vmem, vmem, pl.BlockSpec(memory_space=pl.ANY)],
+        out_specs=(vmem, vmem, vmem),
+        scratch_shapes=[dma((2, chips)), dma((2, chips)), dma((2, chips)), dma((2, chips)), dma((3,))]
+        + [dma((experts,)), dma((experts,))],
         compiler_params=pltpu.CompilerParams(collective_id=0, has_side_effects=True),
-    )(keys, values)
+    )(keys, values, w_out)
     rows = blocks * keys.shape[0]
-    return k_all.reshape(rows, keys.shape[1]), v_all.reshape(rows, keys.shape[1])
+    return k_all.reshape(rows, keys.shape[1]), v_all.reshape(rows, keys.shape[1]), w_part
+
+
+def heads_kernel(experts, x_ref, o_ref, send, recv, local):
+    group = lax.axis_index("expert")
+    cols = x_ref.shape[1]
+
+    def place(g):
+        return o_ref.at[:, pl.ds(pl.multiple_of(g * cols, 128), cols)]
+
+    def push(k, slot):
+        return remote(
+            x_ref, place(slot), send.at[k], recv.at[k], (group + k) % experts, "expert"
+        )
+
+    enter(0, 0, 0, experts)
+    for k in range(experts - 1, 0, -1):
+        push(k, group).start()
+    own = pltpu.make_async_copy(x_ref, place(group), local)
+    own.start()
+    own.wait()
+    for k in range(1, experts):
+        push(k, (group + experts - k) % experts).wait_recv()
+        push(k, group).wait_send()
+
+
+def gather_heads(attended):
+    experts = lax.axis_size("expert")
+    vmem = pl.BlockSpec(memory_space=pltpu.VMEM)
+    dma = pltpu.SemaphoreType.DMA
+    rows, cols = attended.shape
+    return pl.pallas_call(
+        functools.partial(heads_kernel, experts),
+        out_shape=jax.ShapeDtypeStruct((rows, cols * experts), attended.dtype),
+        in_specs=[vmem],
+        out_specs=vmem,
+        scratch_shapes=[dma((experts,)), dma((experts,)), dma],
+        compiler_params=pltpu.CompilerParams(collective_id=2, has_side_effects=True),
+    )(attended)
+
+
+def mix_kernel(
+    experts, att_ref, w_ref, res_ref, gain_ref, router_ref, place_ref, stream_ref, buf_ref, logit_ref,
+    squares, logits, chosen, s_send, s_recv, l_send, l_recv, d_send, d_recv,
+):
+    group = lax.axis_index("expert")
+    rows, cols = res_ref.shape
+
+    def target(k):
+        return (group + k) % experts
+
+    def share_squares(k):
+        return remote(
+            squares.at[0], squares.at[k], s_send.at[k], s_recv.at[k], target(k), "expert"
+        )
+
+    def share_logits(k):
+        return remote(logits.at[0], logits.at[k], l_send.at[k], l_recv.at[k], target(k), "expert")
+
+    def slot(g):
+        return pl.ds(pl.multiple_of(g * cols, 128), cols)
+
+    def dispatch(k, g):
+        return remote(
+            chosen.at[k], buf_ref.at[:, slot(g)], d_send.at[k], d_recv.at[k], target(k), "expert"
+        )
+
+    stream = res_ref[...].astype(jnp.float32) + jnp.dot(
+        att_ref[...], w_ref[...], preferred_element_type=jnp.float32
+    )
+    stream_ref[...] = stream
+    total = jnp.sum(stream * stream, axis=-1, keepdims=True)
+    squares[0] = jnp.transpose(jnp.broadcast_to(total, (rows, 128)))[:8, :]
+    enter(0, 0, 0, experts)
+    for k in range(1, experts):
+        share_squares(k).start()
+    for k in range(1, experts):
+        share_squares(k).wait_recv()
+    total = squares[0]
+    for k in range(1, experts):
+        total = total + squares[k]
+    total = jnp.transpose(jnp.broadcast_to(total[:1, :], (128, rows)))[:, :1]
+    scale = lax.rsqrt(total * (1.0 / (cols * experts)) + 1e-05)
+    normed = (stream_ref[...] * scale * gain_ref[...]).astype(jnp.bfloat16)
+    for k in range(experts - 1, 0, -1):
+        chosen[k] = jnp.dot(
+            place_ref[target(k)], normed, preferred_element_type=jnp.float32
+        ).astype(jnp.bfloat16)
+        dispatch(k, group).start()
+    logits[0] = lax.dot_general(
+        router_ref[...], normed, (((1,), (1,)), ((), ())), preferred_element_type=jnp.float32
+    )
+    for k in range(1, experts):
+        share_logits(k).start()
+    buf_ref[:, slot(group)] = jnp.dot(
+        place_ref[group], normed, preferred_element_type=jnp.float32
+    ).astype(jnp.bfloat16)
+    for k in range(1, experts):
+        share_logits(k).wait_recv()
+    total = logits[0]
+    for k in range(1, experts):
+        total = total + logits[k]
+    logit_ref[...] = total
+    for k in range(1, experts):
+        dispatch(k, target(experts - k)).wait_recv()
+    for k in range(1, experts):
+        share_squares(k).wait_send()
+        share_logits(k).wait_send()
+        dispatch(k, group).wait_send()
+
+
+def mix_columns(attended, w_cols, residual, gain, router, placing):
+    experts = lax.axis_size("expert")
+    rows, cols = residual.shape
+    capacity = placing.shape[1]
+    vmem = pl.BlockSpec(memory_space=pltpu.VMEM)
+    dma = pltpu.SemaphoreType.DMA
+    shape = jax.ShapeDtypeStruct
+    return pl.pallas_call(
+        functools.partial(mix_kernel, experts),
+        out_shape=(
+            shape((rows, cols), jnp.float32),
+            shape((capacity, cols * experts), jnp.bfloat16),
+            shape((router.shape[0], rows), jnp.float32),
+        ),
+        in_specs=[vmem] * 6,
+        out_specs=(vmem, vmem, vmem),
+        scratch_shapes=[
+            pltpu.VMEM((experts, 8, rows), jnp.float32),
+            pltpu.VMEM((experts, router.shape[0], rows), jnp.float32),
+            pltpu.VMEM((experts, capacity, cols), jnp.bfloat16),
+        ]
+        + [dma((experts,)) for _ in range(6)],
+        compiler_params=pltpu.CompilerParams(
+            collective_id=3, has_side_effects=True, vmem_limit_bytes=40 * 1024 * 1024
+        ),
+    )(attended, w_cols, residual, gain, router, placing)
+
+
+def combine_kernel(
+    experts, eo_ref, stream_ref, place_ref, share_ref, o_ref,
+    low, arrived, final, e_send, e_recv, f_send, f_recv, local,
+):
+    group = lax.axis_index("expert")
+    rows, cols = stream_ref.shape
+    own_rows = rows // experts
+
+    def target(k):
+        return (group + k) % experts
+
+    def slot(g):
+        return pl.ds(pl.multiple_of(g * cols, 128), cols)
+
+    def strip(g):
+        return pl.ds(pl.multiple_of(g * own_rows, own_rows), own_rows)
+
+    def give(k, g):
+        return remote(
+            low.at[:, slot(target(k))], arrived.at[g], e_send.at[k], e_recv.at[k], target(k), "expert"
+        )
+
+    def finish(k, g):
+        return remote(
+            final.at[strip(target(k)), :], o_ref.at[:, slot(g)], f_send.at[k], f_recv.at[k],
+            target(k), "expert",
+        )
+
+    low[...] = eo_ref[...].astype(jnp.bfloat16)
+    enter(0, 0, 0, experts)
+    for k in range(experts - 1, 0, -1):
+        give(k, group).start()
+    own = pltpu.make_async_copy(low.at[:, slot(group)], arrived.at[group], local.at[0])
+    own.start()
+    own.wait()
+    for k in range(1, experts):
+        give(k, target(experts - k)).wait_recv()
+    total = stream_ref[...]
+    for g in range(experts):
+        total = total + share_ref[:, g : g + 1] * jnp.dot(
+            place_ref[g], arrived[g], preferred_element_type=jnp.float32
+        )
+    final[...] = total.astype(jnp.bfloat16)
+    for k in range(experts - 1, 0, -1):
+        finish(k, group).start()
+    own = pltpu.make_async_copy(final.at[strip(group), :], o_ref.at[:, slot(group)], local.at[1])
+    own.start()
+    own.wait()
+    for k in range(1, experts):
+        finish(k, target(experts - k)).wait_recv()
+    for k in range(1, experts):
+        give(k, group).wait_send()
+        finish(k, group).wait_send()
+
+
+def combine(expert_out, stream, placing, shares):
+    experts = lax.axis_size("expert")
+    rows, cols = stream.shape
+    capacity = expert_out.shape[0]
+    vmem = pl.BlockSpec(memory_space=pltpu.VMEM)
+    dma = pltpu.SemaphoreType.DMA
+    return pl.pallas_call(
+        functools.partial(combine_kernel, experts),
+        out_shape=jax.ShapeDtypeStruct((rows // experts, cols * experts), jnp.bfloat16),
+        in_specs=[vmem] * 4,
+        out_specs=vmem,
+        scratch_shapes=[
+            pltpu.VMEM((capacity, cols * experts), jnp.bfloat16),
+            pltpu.VMEM((experts, capacity, cols), jnp.bfloat16),
+            pltpu.VMEM((rows, cols), jnp.bfloat16),
+        ]
+        + [dma((experts,)) for _ in range(4)]
+        + [dma((2,))],
+        compiler_params=pltpu.CompilerParams(
+            collective_id=4, has_side_effects=True, vmem_limit_bytes=40 * 1024 * 1024
+        ),
+    )(expert_out, stream, placing, shares)
 
 
 def expert_kernel(
@@ -285,14 +535,15 @@
     q_per_kv = H // KVH
     seq_block = lax.axis_index("blk")
     head_group = lax.axis_index("expert")
-    group_count = lax.axis_size("expert")
     first_row = seq_block * tok_rows
     query_pos = first_row + jnp.arange(tok_rows, dtype=jnp.int32)
     query_seg = lax.dynamic_slice_in_dim(segments, first_row, tok_rows)
     query_four = queries.reshape(tok_rows, kv_heads, q_per_kv, HD)
     score_scale = 1.0 / math.sqrt(HD)
     running = jnp.full((kv_heads, q_per_kv, tok_rows), -1e30, jnp.float32)
-    key_rows, value_rows = gather_blocks(key_cache, value_cache)
+    key_rows, value_rows, w_part = gather_blocks(key_cache, value_cache, w_out)
+    w_cols = lax.all_gather(w_part, "blk", axis=1, tiled=True)
+    w_cols = w_cols.reshape(-1, w_cols.shape[2])
     piece_len = key_rows.shape[0]
     key_pos = jnp.arange(piece_len, dtype=jnp.int32)
     visible = (query_seg[:, None] == segments[None, :]) & (key_pos[None, :] <= query_pos[:, None])
@@ -321,42 +572,29 @@
         .reshape(tok_rows, kv_heads * q_per_kv * HD)
         .astype(jnp.bfloat16)
     )
-    head_term = jnp.dot(attended, w_out, preferred_element_type=jnp.float32)
     feat_width = residual.shape[1]
-    own_cols = lax.dynamic_slice_in_dim(
-        head_term, head_group * feat_width, feat_width, 1
-    ) + residual.astype(jnp.float32)
-    head_term = lax.dynamic_update_slice_in_dim(head_term, own_cols, head_group * feat_width, 1)
-    row_share = tok_rows // group_count
-    summed = lax.psum(head_term.astype(jnp.bfloat16), "expert").astype(jnp.float32)
-    normed = (
-        summed * lax.rsqrt(jnp.mean(summed * summed, axis=-1, keepdims=True) + 1e-05) * norm_gain
-    ).astype(jnp.bfloat16)
-    own_rows = lax.dynamic_slice_in_dim(summed, head_group * row_share, row_share, 0)
-    gate_score = jax.nn.sigmoid(jnp.dot(normed, w_router, preferred_element_type=jnp.float32))
-    picked = routes[:, :, None] == jnp.arange(w_router.shape[1], dtype=jnp.int32)[None, None, :]
-    chosen = jnp.sum(jnp.where(picked, gate_score[:, None, :], 0.0), axis=-1)
-    mixing = chosen / jnp.sum(chosen, axis=-1, keepdims=True)
-    expert_id = head_group * w_gate.shape[0]
-    chosen_here = routes == expert_id
-    routed = jnp.any(chosen_here, axis=-1)
-    share_w = jnp.sum(jnp.where(chosen_here, mixing, 0.0), axis=-1)
-    capacity = tok_rows * TOP * 9 // (8 * w_gate.shape[0] * group_count)
+    experts = w_router.shape[1]
+    first_col = head_group * feat_width
+    capacity = tok_rows * TOP * 9 // (8 * experts)
     capacity = -(-capacity // 16) * 16
-    slot_index = jnp.cumsum(routed.astype(jnp.int32)) - 1
-    placing = (
-        (slot_index[None, :] == jnp.arange(capacity, dtype=jnp.int32)[:, None]) & routed[None, :]
-    ).astype(jnp.bfloat16)
-    buffer = jnp.dot(placing, normed, preferred_element_type=jnp.float32).astype(jnp.bfloat16)
-    gate_w = w_gate[0]
-    up_w = w_up[0]
-    down_w = w_down[0]
-    expert_out = expert_layer(buffer, gate_w, up_w, down_w)
-    contrib = jnp.take(expert_out, jnp.clip(slot_index, 0, capacity - 1), axis=0) * share_w[:, None]
-    combined = lax.psum_scatter(
-        contrib.astype(jnp.bfloat16), "expert", scatter_dimension=0, tiled=True
-    ).astype(jnp.float32)
-    return (own_rows + combined).astype(jnp.bfloat16)
+    ids = jnp.arange(experts, dtype=jnp.int32)
+    picked = routes[:, :, None] == ids[None, None, :]
+    routed = jnp.any(picked, axis=1).T
+    slot_index = jnp.where(routed, jnp.cumsum(routed.astype(jnp.int32), axis=1) - 1, -1)
+    slots = jnp.arange(capacity, dtype=jnp.int32)
+    placing = (slot_index[:, None, :] == slots[None, :, None]).astype(jnp.bfloat16)
+    placing_back = (slot_index[:, :, None] == slots[None, None, :]).astype(jnp.bfloat16)
+    router = lax.dynamic_slice_in_dim(w_router, first_col, feat_width, 0).T
+    router = jnp.pad(router, ((0, -experts % 16), (0, 0)))
+    gain = lax.dynamic_slice_in_dim(norm_gain, first_col, feat_width)[None, :]
+    attended = gather_heads(attended)
+    stream, buffer, logits = mix_columns(attended, w_cols, residual, gain, router, placing)
+    gate_score = jax.nn.sigmoid(logits[:experts, :].T)
+    chosen = jnp.where(routed.T, gate_score, 0.0)
+    shares = chosen / jnp.sum(chosen, axis=-1, keepdims=True)
+    shares = jnp.pad(shares, ((0, 0), (0, -experts % 128)))
+    expert_out = expert_layer(buffer, w_gate[0], w_up[0], w_down[0])
+    return combine(expert_out, stream, placing_back, shares)
 
 
 def solution(mesh):

time: 357 us -> 306 us (0.86)
  waiting for transfers between devices: 127 us -> 0.04 us
  Pallas kernels: 166 us -> 270 us
  other arithmetic: 23.8 us -> 4.5 us
  matrix products: 14.5 us -> 3.89 us
    pallas_call x1 -> x4, Pallas kernels: 20.1 us -> 126 us  [the longest x1 41 us: combine(): pl.pallas_call(functools.partial(combine_kernel, experts), out_shape=jax....]
    psum x1 -> x0, waiting for transfers between devices: 86.6 us -> none  [on_device(): lax.psum(head_term.astype(jnp.bfloat16), 'expert').astype(jnp.float32)]
    reduce_scatter x1 -> x0, waiting for transfers between devices: 40.1 us -> none  [on_device(): lax.psum_scatter(contrib.astype(jnp.bfloat16), 'expert', scatter_dimensio...]
    convert_element_type x5 -> x2, other arithmetic: 12.7 us -> 0.27 us  [the longest x1 0.2 us: on_device(): (slot_index[:, :, None] == slots[None, None, :]).astype(jnp.bfloat16)]
    dot_general x3 -> x0, matrix products: 7.41 us -> none  [the longest x1 3.25 us: on_device(): head_term = jnp.dot(attended, w_out, preferred_element_type=jnp.float32)]
    gather x1 -> x0, local copies, waits for them, and re-layouts: 7.28 us -> none  [on_device(): jnp.take(expert_out, jnp.clip(slot_index, 0, capacity - 1), axis=0)]
    unnamed x18 -> x19, local copies, waits for them, and re-layouts: 1.22 us -> 6.9 us
  transfers between devices with their start and end apart: 2 -> 1, of which waited for: 2 -> 0; matrix products, arithmetic and copies ran while one was open for 1% -> 5% of each run, Pallas kernels for 0% -> 9%
where the time goes in v2:
time: 306 us; the launch traced here: 305 us
  Pallas kernels  270 us (88%)
  between operations  13.6 us (4%)
  local copies, waits for them, and re-layouts  12.9 us (4%)
  other arithmetic  4.5 us (1%)
  matrix products  3.89 us (1%)
    pallas_call x1, Pallas kernels, expert_layer(): pl.pallas_call(functools.partial(expert_kernel, chips, tiles), grid=(chip...  144 us
    pallas_call x1, Pallas kernels, combine(): pl.pallas_call(functools.partial(combine_kernel, experts), out_shape=jax....  41 us
    pallas_call x1, Pallas kernels, mix_columns(): pl.pallas_call(functools.partial(mix_kernel, experts), out_shape=(shape((...  34.4 us
    pallas_call x1, Pallas kernels, gather_heads(): pl.pallas_call(functools.partial(heads_kernel, experts), out_shape=jax.Sh...  28.4 us
    pallas_call x1, Pallas kernels, gather_blocks(): pl.pallas_call(functools.partial(gather_kernel, chips, experts), out_shap...  22.4 us
    unnamed x19, local copies, waits for them, and re-layouts  6.9 us
  transfers between devices with their start and end apart: 1, of which 0 were waited for; matrix products, arithmetic and copies ran while one was open for 5% of the time, Pallas kernels for 9%

profile of v2, /device:TPU:0, one launch (start us, length us, event | category | flops | bytes accessed | tf_op | source)
XLA Modules:
  0.0 305.3 jit_solution(1561014964235711081)
XLA Ops:
  6.5 0.0 copy-start
  6.5 0.0 copy-start.7
  6.5 0.0 all-gather.2.cloned.1.call-start
  6.5 22.4 %shard_map.118 = (bf16[8,256,256]{2,1,0:T(8,128)(2,1)}, bf16[8,256,256]{2,1,0:T(8,128)(2,1)}, bf16[4,64,1024]{2,1,0:T(8,128)(2,1)}) custom-call(bf16[256,256]{1,0:T(8,128)(2,1)} %k_ref.1, bf16[256,256]{1,0:T(8,128)(2,1)} %v_ref.1, bf16[512,4096]{1,0:T(8,128)(2,1)} %w_ref.1), custom_call_target="tpu_custom_call" | custom-call | tf_op jit(solution)/shard_map/pallas_call | solution.py:116
  29.0 0.0 all-gather.2.cloned.1.call-update
  29.0 1.3 reshape_reshape.6
  30.3 1.0 reshape.35
  31.4 1.3 reshape_reshape.7
  32.7 0.0 copy-done.7
  32.7 0.1 dynamic_slice.9
  32.8 0.5 fusion.6
  33.4 1.5 fusion
  34.9 2.1 fusion.1
  37.0 0.0 copy-start.8
  37.0 0.0 copy-start.6
  37.0 2.4 fusion.19
  39.4 0.8 copy.53.x_ref
  40.2 28.4 %shard_map.119.att_ref = bf16[256,2048]{1,0:T(8,128)(2,1)} custom-call(bf16[256,512]{1,0:T(8,128)(2,1)} %copy.53.x_ref), custom_call_target="tpu_custom_call" | custom-call | tf_op jit(solution)/shard_map/pallas_call | solution.py:157
  68.6 0.0 copy-done.8
  68.7 0.2 copy.45
  68.9 1.2 reduce-window.6
  70.1 0.1 slice.12
  70.2 0.1 copy.40
  70.3 0.1 copy.41
  70.4 0.7 dynamic_slice.10
  71.1 0.0 copy-done
  71.1 0.1 add_bitcast_fusion
  71.2 0.1 fusion.24.place_ref
  71.3 0.2 fusion.13.place_ref
  71.5 0.0 all-gather.2.cloned.1.call-done
  71.5 0.0 copy-done.6
  71.5 0.0 copy-start.3
  71.5 2.2 copy-done.3
  73.7 0.0 copy-start.4
  73.7 1.2 copy-done.4
  75.0 34.4 %shard_map.120 = (f32[256,1024]{1,0:T(8,128)S(1)}, bf16[144,4096]{1,0:T(8,128)(2,1)S(1)}, f32[16,256]{1,0:T(8,128)S(1)}) custom-call(bf16[256,2048]{1,0:T(8,128)(2,1)S(1)} %copy-done.4, bf16[2048,1024]{1,0:T(8,128)(2,1)S(1)} %bitcast.48, bf16[256,1024]{1,0:T(8,128)(2,1)S(1)} %copy-done.6, f32[1,1024]{1,0:T(1,128)S(1)} %bitcast.49, ...), custom_call_target="tpu_custom_call" | custom-call | tf_op jit(solution)/shard_map/pallas_call | solution.py:244
  109.4 0.0 copy-start.5
  109.4 1.0 copy-done.5
  110.4 0.1 copy.42
  110.5 0.1 fusion.27
  110.7 0.1 broadcast_divide_fusion
  110.8 0.0 copy-start.1
  110.8 144.1 %shard_map.121.eo_ref = f32[144,4096]{1,0:T(8,128)} custom-call(bf16[144,4096]{1,0:T(8,128)(2,1)} %copy-done.5, bf16[4096,1792]{1,0:T(8,128)(2,1)} %bitcast.50, bf16[4096,1792]{1,0:T(8,128)(2,1)} %bitcast.51, bf16[1792,4096]{1,0:T(8,128)(2,1)} %bitcast.52), custom_call_target="tpu_custom_call" | custom-call | tf_op jit(solution)/shard_map/pallas_call | solution.py:489
  254.9 0.0 copy-start.2
  254.9 1.7 copy-done.2
  256.6 41.0 %shard_map.122 = bf16[64,4096]{1,0:T(8,128)(2,1)S(1)} custom-call(f32[144,4096]{1,0:T(8,128)S(1)} %copy-done.2, f32[256,1024]{1,0:T(8,128)S(1)} %get-tuple-element.15.stream_ref, bf16[4,256,144]{2,1,0:T(8,128)(2,1)S(1)} %fusion.13.place_ref, f32[256,128]{1,0:T(8,128)S(1)} %pad.9.share_ref), custom_call_target="tpu_custom_call" | custom-call | tf_op jit(solution)/shard_map/pallas_call | solution.py:326
  297.6 0.8 copy.71
  298.4 0.0 copy-done.1
  (12 shorter events, 0.1 us)
Async XLA Ops:
  6.5 64.6 %copy-start = (bf16[4096,4]{0,1:T(4,128)(2,1)S(1)}, bf16[4096,4]{0,1:T(4,128)(2,1)}, u32[]{:S(2)}) copy-start(bf16[4096,4]{0,1:T(4,128)(2,1)} %param.20) | copy-start | bytes 98308
  6.5 26.2 %copy-start.7 = (s32[2048]{0:T(1024)S(1)}, s32[2048]{0:T(1024)}, u32[]{:S(2)}) copy-start(s32[2048]{0:T(1024)} %param.16) | copy-start | bytes 24580
  6.5 65.0 %all-gather.2.cloned.1.call-start = ((), (), s32[]{:S(2)}) async-start(), calls=%async_computation | async-start | bytes 4718592 | tf_op jit(solution)/shard_map/all_gather | solution.py:545
  37.0 31.7 %copy-start.8 = (s32[256,2]{0,1:T(2,128)S(1)}, s32[256,2]{0,1:T(2,128)}, u32[]{:S(2)}) copy-start(s32[256,2]{0,1:T(2,128)} %param.17) | copy-start | bytes 6148
  37.0 34.5 %copy-start.6 = (bf16[256,1024]{1,0:T(8,128)(2,1)S(1)}, bf16[256,1024]{1,0:T(8,128)(2,1)}, u32[]{:S(2)}) copy-start(bf16[256,1024]{1,0:T(8,128)(2,1)} %res_ref.1) | copy-start | bytes 1572868
  71.5 2.2 copy-start.3
  73.7 1.2 copy-start.4
  109.4 1.0 copy-start.5
  110.8 187.6 %copy-start.1 = (bf16[4096,4]{0,1:T(4,128)(2,1)S(1)}, bf16[4096,4]{0,1:T(4,128)(2,1)}, u32[]{:S(2)}) copy-start(bf16[4096,4]{0,1:T(4,128)(2,1)} %param.20) | copy-start | bytes 98308
  254.9 1.7 copy-start.2
Sparse Core Ops, SparseCore 0:
  29.1 35.4 all-gather.1

commit v3 on v2

--- a/solution.py
+++ b/solution.py
@@ -341,16 +341,21 @@
     )(expert_out, stream, placing, shares)
 
 
+SPAN = 512
+PARTS = 4
+
+
 def expert_kernel(
     chips,
     tiles,
+    spans,
     x_ref,
     wg_ref,
     wu_ref,
     wd_ref,
     o_ref,
     rows_in,
-    acc,
+    hidden,
     keep,
     leaving,
     sib_in,
@@ -370,7 +375,9 @@
     chip, core = me // 2, me % 2
     sibling = chip * 2 + 1 - core
     rows, width = x_ref.shape
-    mid = min(2, tiles - 1)
+    tile = wg_ref.shape[1]
+    per_part = spans // PARTS
+    wide = width // PARTS
 
     def push(k):
         return remote(
@@ -380,12 +387,18 @@
     def forward(k):
         return remote(rows_in.at[k, 0], rows_in.at[k, 1], fw_send.at[k], fw_recv.at[k], sibling)
 
-    def exchange(k):
-        return remote(leaving.at[k % 2], sib_in.at[k], sib_send.at[k], sib_recv.at[k], sibling)
-
-    def deliver(k):
-        return remote(
-            sib_in.at[k], part_in.at[k], rs_send.at[k], rs_recv.at[k], (chip + chips - k) % chips * 2 + core
+    def exchange(k, q):
+        return remote(
+            leaving.at[k % 2, q], sib_in.at[k, q], sib_send.at[k, q], sib_recv.at[k, q], sibling
+        )
+
+    def deliver(k, q):
+        return remote(
+            sib_in.at[k, q],
+            part_in.at[k, q],
+            rs_send.at[k, q],
+            rs_recv.at[k, q],
+            (chip + chips - k) % chips * 2 + core,
         )
 
     @pl.when((j == 0) & (f == 0))
@@ -406,75 +419,83 @@
     def _():
         forward(j).wait_recv()
 
-    tokens = rows_in[j].reshape(2 * rows, width)
-    gate = jnp.dot(tokens, wg_ref[...], preferred_element_type=jnp.float32)
-    up = jnp.dot(tokens, wu_ref[...], preferred_element_type=jnp.float32)
-    hidden = (gate / (1.0 + jnp.exp(-gate)) * up).astype(jnp.bfloat16)
-    step = 1024
-
-    @pl.when(f == 0)
-    def _():
-        for c in range(0, width, step):
-            acc[:, c : c + step] = jnp.dot(
-                hidden, wd_ref[:, c : c + step], preferred_element_type=jnp.float32
-            )
-
-    @pl.when(f > 0)
-    def _():
-        for c in range(0, width, step):
-            acc[:, c : c + step] += jnp.dot(
-                hidden, wd_ref[:, c : c + step], preferred_element_type=jnp.float32
-            )
-
-    @pl.when((f == mid) & (j + 1 < chips))
+    def settle(k, q):
+        exchange(k, q).wait_recv()
+        part = pl.ds(pl.multiple_of(q * wide, wide), wide)
+
+        @pl.when(k == 0)
+        def _():
+            o_ref[:, part] += sib_in[k, q].astype(jnp.float32)
+
+        @pl.when(k > 0)
+        def _():
+            sib_in[k, q] = (keep[:, part] + sib_in[k, q].astype(jnp.float32)).astype(jnp.bfloat16)
+            deliver(k, q).start()
+
+    @pl.when((f == 1) & (j >= 1))
+    def _():
+        settle(j - 1, PARTS - 1)
+
+    @pl.when(f < tiles)
+    def _():
+        tokens = rows_in[j].reshape(2 * rows, width)
+        gate = jnp.dot(tokens, wg_ref[...], preferred_element_type=jnp.float32)
+        up = jnp.dot(tokens, wu_ref[...], preferred_element_type=jnp.float32)
+        hidden[:, pl.ds(pl.multiple_of(f * tile, tile), tile)] = (
+            gate / (1.0 + jnp.exp(-gate)) * up
+        ).astype(jnp.bfloat16)
+
+    @pl.when((f == tiles // 2) & (j + 1 < chips))
     def _():
         push(j + 1).wait_recv()
         forward(j + 1).start()
 
-    def settle(k):
-        exchange(k).wait_recv()
-        sib_in[k] = (keep[...] + sib_in[k].astype(jnp.float32)).astype(jnp.bfloat16)
-        deliver(k).start()
-
-    @pl.when((f == 1) & (j == 1))
-    def _():
-        exchange(0).wait_recv()
-        o_ref[...] += sib_in[0].astype(jnp.float32)
-
-    @pl.when((f == 1) & (j >= 2))
-    def _():
-        settle(j - 1)
-
-    @pl.when(f == tiles - 1)
-    def _():
-        @pl.when(j >= 2)
+    @pl.when(f >= tiles)
+    def _():
+        n = f - tiles
+        q, r = n // per_part, n % per_part
+
+        @pl.when((j >= 2) & (r == 0))
         def _():
-            exchange(j - 2).wait_send()
-
-        leaving[j % 2] = acc[rows:, :].astype(jnp.bfloat16)
-        exchange(j).start()
+            exchange(j - 2, q).wait_send()
+
+        result = jnp.dot(hidden[...], wd_ref[...], preferred_element_type=jnp.float32)
+        inner = pl.ds(pl.multiple_of(r * SPAN, SPAN), SPAN)
+        outer = pl.ds(pl.multiple_of(n * SPAN, SPAN), SPAN)
+        leaving[j % 2, q, :, inner] = result[rows:, :].astype(jnp.bfloat16)
 
         @pl.when(j == 0)
         def _():
-            o_ref[...] = acc[:rows, :]
+            o_ref[:, outer] = result[:rows, :]
 
         @pl.when(j > 0)
         def _():
-            keep[...] = acc[:rows, :]
-
-        @pl.when(j == chips - 1)
+            keep[:, outer] = result[:rows, :]
+
+        @pl.when(r == per_part - 1)
         def _():
-            settle(chips - 1)
-            for k in range(1, chips):
-                deliver(k).wait_recv()
-                o_ref[...] += part_in[k].astype(jnp.float32)
-            for k in range(chips):
-                forward(k).wait_send()
-                if k >= 1:
-                    push(k).wait_send()
-                    deliver(k).wait_send()
-            for k in range(max(0, chips - 2), chips):
-                exchange(k).wait_send()
+            exchange(j, q).start()
+
+            @pl.when(q >= 1)
+            def _():
+                settle(j, q - 1)
+
+    @pl.when((j == chips - 1) & (f == tiles + spans - 1))
+    def _():
+        settle(chips - 1, PARTS - 1)
+        for k in range(1, chips):
+            for q in range(PARTS):
+                deliver(k, q).wait_recv()
+                o_ref[:, q * wide : (q + 1) * wide] += part_in[k, q].astype(jnp.float32)
+        for k in range(chips):
+            forward(k).wait_send()
+            if k >= 1:
+                push(k).wait_send()
+                for q in range(PARTS):
+                    deliver(k, q).wait_send()
+        for k in range(max(0, chips - 2), chips):
+            for q in range(PARTS):
+                exchange(k, q).wait_send()
 
 
 def expert_layer(x, gate_w, up_w, down_w):
@@ -484,28 +505,30 @@
     units = gate_w.shape[1]
     tile = 256 if units % 256 == 0 else 128
     tiles = units // tile
+    spans = width // SPAN
     dma = pltpu.SemaphoreType.DMA
     low, wide = jnp.bfloat16, jnp.float32
     return pl.pallas_call(
-        functools.partial(expert_kernel, chips, tiles),
-        grid=(chips, tiles),
+        functools.partial(expert_kernel, chips, tiles, spans),
+        grid=(chips, tiles + spans),
         out_shape=jax.ShapeDtypeStruct((rows, width), wide),
         in_specs=[
             pl.BlockSpec(memory_space=pl.ANY),
-            pl.BlockSpec((width, tile), lambda j, f: (0, f)),
-            pl.BlockSpec((width, tile), lambda j, f: (0, f)),
-            pl.BlockSpec((tile, width), lambda j, f: (f, 0)),
+            pl.BlockSpec((width, tile), lambda j, f: (0, jnp.minimum(f, tiles - 1))),
+            pl.BlockSpec((width, tile), lambda j, f: (0, jnp.minimum(f, tiles - 1))),
+            pl.BlockSpec((units, SPAN), lambda j, f: (0, jnp.maximum(f - tiles, 0))),
         ],
         out_specs=pl.BlockSpec((rows, width), lambda j, f: (0, 0)),
         scratch_shapes=[
             pltpu.VMEM((chips, 2, rows, width), low),
-            pltpu.VMEM((2 * rows, width), wide),
+            pltpu.VMEM((2 * rows, units), low),
             pltpu.VMEM((rows, width), wide),
-            pltpu.VMEM((2, rows, width), low),
-            pltpu.VMEM((chips, rows, width), low),
-            pltpu.VMEM((chips, rows, width), low),
+            pltpu.VMEM((2, PARTS, rows, width // PARTS), low),
+            pltpu.VMEM((chips, PARTS, rows, width // PARTS), low),
+            pltpu.VMEM((chips, PARTS, rows, width // PARTS), low),
         ]
-        + [dma((chips,)) for _ in range(8)]
+        + [dma((chips,)) for _ in range(4)]
+        + [dma((chips, PARTS)) for _ in range(4)]
         + [dma],
         compiler_params=pltpu.CompilerParams(
             collective_id=1,

time: 306 us -> 306 us (level)
  no operation moved by 1% of the time
where the time goes in v3:
time: 306 us; the launch traced here: 305 us
  Pallas kernels  270 us (88%)
  between operations  13.6 us (4%)
  local copies, waits for them, and re-layouts  12.9 us (4%)
  other arithmetic  4.5 us (1%)
  matrix products  3.89 us (1%)
    pallas_call x1, Pallas kernels, expert_layer(): pl.pallas_call(functools.partial(expert_kernel, chips, tiles, spans), gri...  144 us
    pallas_call x1, Pallas kernels, combine(): pl.pallas_call(functools.partial(combine_kernel, experts), out_shape=jax....  41 us
    pallas_call x1, Pallas kernels, mix_columns(): pl.pallas_call(functools.partial(mix_kernel, experts), out_shape=(shape((...  34.4 us
    pallas_call x1, Pallas kernels, gather_heads(): pl.pallas_call(functools.partial(heads_kernel, experts), out_shape=jax.Sh...  28.4 us
    pallas_call x1, Pallas kernels, gather_blocks(): pl.pallas_call(functools.partial(gather_kernel, chips, experts), out_shap...  22.4 us
    unnamed x19, local copies, waits for them, and re-layouts  6.9 us
  transfers between devices with their start and end apart: 1, of which 0 were waited for; matrix products, arithmetic and copies ran while one was open for 5% of the time, Pallas kernels for 9%

profile of v3, /device:TPU:0, one launch (start us, length us, event | category | flops | bytes accessed | tf_op | source)
XLA Modules:
  0.0 305.1 jit_solution(3644200128781618075)
XLA Ops:
  6.5 0.0 copy-start
  6.5 0.0 copy-start.7
  6.5 0.0 all-gather.2.cloned.1.call-start
  6.5 22.4 %shard_map.118 = (bf16[8,256,256]{2,1,0:T(8,128)(2,1)}, bf16[8,256,256]{2,1,0:T(8,128)(2,1)}, bf16[4,64,1024]{2,1,0:T(8,128)(2,1)}) custom-call(bf16[256,256]{1,0:T(8,128)(2,1)} %k_ref.1, bf16[256,256]{1,0:T(8,128)(2,1)} %v_ref.1, bf16[512,4096]{1,0:T(8,128)(2,1)} %w_ref.1), custom_call_target="tpu_custom_call" | custom-call | tf_op jit(solution)/shard_map/pallas_call | solution.py:116
  29.0 0.0 all-gather.2.cloned.1.call-update
  29.0 1.3 reshape_reshape.6
  30.3 1.0 reshape.35
  31.4 1.3 reshape_reshape.7
  32.7 0.0 copy-done.7
  32.7 0.1 dynamic_slice.9
  32.8 0.5 fusion.6
  33.4 1.5 fusion
  34.9 2.1 fusion.1
  37.0 0.0 copy-start.8
  37.0 0.0 copy-start.6
  37.0 2.4 fusion.19
  39.4 0.8 copy.53.x_ref
  40.2 28.4 %shard_map.119.att_ref = bf16[256,2048]{1,0:T(8,128)(2,1)} custom-call(bf16[256,512]{1,0:T(8,128)(2,1)} %copy.53.x_ref), custom_call_target="tpu_custom_call" | custom-call | tf_op jit(solution)/shard_map/pallas_call | solution.py:157
  68.6 0.0 copy-done.8
  68.7 0.2 copy.45
  68.9 1.2 reduce-window.6
  70.1 0.1 slice.12
  70.2 0.1 copy.40
  70.3 0.1 copy.41
  70.4 0.7 dynamic_slice.10
  71.1 0.0 copy-done
  71.1 0.1 add_bitcast_fusion
  71.2 0.1 fusion.24.place_ref
  71.3 0.2 fusion.13.place_ref
  71.5 0.0 all-gather.2.cloned.1.call-done
  71.5 0.0 copy-done.6
  71.5 0.0 copy-start.3
  71.6 2.2 copy-done.3
  73.7 0.0 copy-start.4
  73.7 1.2 copy-done.4
  75.0 34.4 %shard_map.120 = (f32[256,1024]{1,0:T(8,128)S(1)}, bf16[144,4096]{1,0:T(8,128)(2,1)S(1)}, f32[16,256]{1,0:T(8,128)S(1)}) custom-call(bf16[256,2048]{1,0:T(8,128)(2,1)S(1)} %copy-done.4, bf16[2048,1024]{1,0:T(8,128)(2,1)S(1)} %bitcast.48, bf16[256,1024]{1,0:T(8,128)(2,1)S(1)} %copy-done.6, f32[1,1024]{1,0:T(1,128)S(1)} %bitcast.49, ...), custom_call_target="tpu_custom_call" | custom-call | tf_op jit(solution)/shard_map/pallas_call | solution.py:244
  109.4 0.0 copy-start.5
  109.4 1.0 copy-done.5
  110.4 0.1 copy.42
  110.5 0.1 fusion.27
  110.7 0.1 broadcast_divide_fusion
  110.8 0.0 copy-start.1
  110.8 144.0 %shard_map.121.eo_ref = f32[144,4096]{1,0:T(8,128)} custom-call(bf16[144,4096]{1,0:T(8,128)(2,1)} %copy-done.5, bf16[4096,1792]{1,0:T(8,128)(2,1)} %bitcast.50, bf16[4096,1792]{1,0:T(8,128)(2,1)} %bitcast.51, bf16[1792,4096]{1,0:T(8,128)(2,1)} %bitcast.52), custom_call_target="tpu_custom_call" | custom-call | tf_op jit(solution)/shard_map/pallas_call | solution.py:511
  254.9 0.0 copy-start.2
  254.9 1.7 copy-done.2
  256.5 41.0 %shard_map.122 = bf16[64,4096]{1,0:T(8,128)(2,1)S(1)} custom-call(f32[144,4096]{1,0:T(8,128)S(1)} %copy-done.2, f32[256,1024]{1,0:T(8,128)S(1)} %get-tuple-element.15.stream_ref, bf16[4,256,144]{2,1,0:T(8,128)(2,1)S(1)} %fusion.13.place_ref, f32[256,128]{1,0:T(8,128)S(1)} %pad.9.share_ref), custom_call_target="tpu_custom_call" | custom-call | tf_op jit(solution)/shard_map/pallas_call | solution.py:326
  297.5 0.8 copy.71
  298.3 0.0 copy-done.1
  (12 shorter events, 0.1 us)
Async XLA Ops:
  6.5 64.6 %copy-start = (bf16[4096,4]{0,1:T(4,128)(2,1)S(1)}, bf16[4096,4]{0,1:T(4,128)(2,1)}, u32[]{:S(2)}) copy-start(bf16[4096,4]{0,1:T(4,128)(2,1)} %param.20) | copy-start | bytes 98308
  6.5 26.2 %copy-start.7 = (s32[2048]{0:T(1024)S(1)}, s32[2048]{0:T(1024)}, u32[]{:S(2)}) copy-start(s32[2048]{0:T(1024)} %param.16) | copy-start | bytes 24580
  6.5 65.0 %all-gather.2.cloned.1.call-start = ((), (), s32[]{:S(2)}) async-start(), calls=%async_computation | async-start | bytes 4718592 | tf_op jit(solution)/shard_map/all_gather | solution.py:568
  37.0 31.7 %copy-start.8 = (s32[256,2]{0,1:T(2,128)S(1)}, s32[256,2]{0,1:T(2,128)}, u32[]{:S(2)}) copy-start(s32[256,2]{0,1:T(2,128)} %param.17) | copy-start | bytes 6148
  37.0 34.5 %copy-start.6 = (bf16[256,1024]{1,0:T(8,128)(2,1)S(1)}, bf16[256,1024]{1,0:T(8,128)(2,1)}, u32[]{:S(2)}) copy-start(bf16[256,1024]{1,0:T(8,128)(2,1)} %res_ref.1) | copy-start | bytes 1572868
  71.5 2.2 copy-start.3
  73.7 1.2 copy-start.4
  109.4 1.0 copy-start.5
  110.8 187.5 %copy-start.1 = (bf16[4096,4]{0,1:T(4,128)(2,1)S(1)}, bf16[4096,4]{0,1:T(4,128)(2,1)}, u32[]{:S(2)}) copy-start(bf16[4096,4]{0,1:T(4,128)(2,1)} %param.20) | copy-start | bytes 98308
  254.9 1.7 copy-start.2
Sparse Core Ops, SparseCore 0:
  29.1 35.4 all-gather.1
